TPU v7x, 32 devices: a whole 2x2x4 slice. The times are simulated.
32 devices in a mesh: ord: 8 (over z, core), gx: 2 (over x), gy: 2 (over y).
Axes of the slice: x: 2, y: 2, z: 4, core: 2. Of those that a mesh axis runs over, the one named last changes fastest.
Arguments:
- distribution: float32 [256, 64, 8, 128], P('ord', 'gx', 'gy'), may hold values from -4.5 to 4.5
- relaxation: float32 [64, 8, 128], P('gx', 'gy'), may hold values from 0.05 to 5
Outputs:
- updated: float32 [256, 64, 8, 128], P('ord', 'gx', 'gy')
- temperature: float32 [64, 8, 128], P('gx', 'gy')
All inputs are finite; a program needn't handle non-finite values.
Results may differ from a plain program's by a relative error of at most 0.0003.
Values sent between devices are 32-bit elements; how exact they have to be, the bound alone decides.
A program may use at most 64 MiB of HBM per device.

v0:
```python
import jax
import jax.numpy as jnp
from jax import lax
from jax.sharding import PartitionSpec as P

NORD = 256
STEPS = 2
SWEEPS = 3
time_step = 0.4
limiter_eps = 0.01
diffusion_mass = 0.5
flux_weight = 2.0
golden_turn = 2.399963229728653


def extended(cells, sides, width):
    for axis, dim in sides:
        count = lax.axis_size(axis)
        ends = count - 1
        head = lax.slice_in_dim(cells, 0, width, axis=dim)
        tail = lax.slice_in_dim(cells, cells.shape[dim] - width, cells.shape[dim], axis=dim)
        cells = jnp.concatenate(
            [
                lax.ppermute(tail, axis, [(i, (i + 1) % count) for i in range(ends)]),
                cells,
                lax.ppermute(head, axis, [((i + 1) % count, i) for i in range(ends)]),
            ],
            axis=dim,
        )
    return cells


def directions(offset, length):
    ordinal = (offset + jnp.arange(length, dtype=jnp.int32)).astype(jnp.float32)
    height = 1.0 - (2.0 * ordinal + 1.0) / NORD
    radius = jnp.sqrt(1.0 - height * height)
    turned = golden_turn * ordinal
    return jnp.stack([radius * jnp.cos(turned), radius * jnp.sin(turned), height])


def window(values, anchor, length, axis_dim):
    return lax.slice_in_dim(values, anchor, anchor + length, axis=axis_dim)


def pad_along(values, width, axis_dim):
    widths = [
        (width, width) if dimension == axis_dim else (0, 0) for dimension in range(values.ndim)
    ]
    return jnp.pad(values, widths)


def source_of(current, local_temp, relax):
    return ((2.0 * relax - time_step) * current + 2.0 * time_step * local_temp) / (
        2.0 * relax + time_step
    )


def axis_flux(padded, temp_pad, relax_pad, along_speed, axis_dim):
    length = padded.shape[axis_dim] - 4
    lower_diff = window(padded, 1, length + 2, axis_dim) - window(padded, 0, length + 2, axis_dim)
    upper_diff = window(padded, 2, length + 2, axis_dim) - window(padded, 1, length + 2, axis_dim)
    centre = window(padded, 1, length + 2, axis_dim)
    slopes = (
        lower_diff * (upper_diff * upper_diff + limiter_eps)
        + upper_diff * (lower_diff * lower_diff + limiter_eps)
    ) / (lower_diff * lower_diff + upper_diff * upper_diff + 2.0 * limiter_eps)
    upwind_low = window(centre, 0, length + 1, axis_dim) + 0.5 * (
        1.0 - time_step * along_speed
    ) * window(slopes, 0, length + 1, axis_dim)
    upwind_high = window(centre, 1, length + 1, axis_dim) - 0.5 * (
        1.0 + time_step * along_speed
    ) * window(slopes, 1, length + 1, axis_dim)
    upwind = jnp.where(along_speed >= 0.0, upwind_low, upwind_high)
    temp_face = 0.5 * (
        window(temp_pad, 0, length + 1, axis_dim) + window(temp_pad, 1, length + 1, axis_dim)
    )
    relax_face = 0.5 * (
        window(relax_pad, 0, length + 1, axis_dim) + window(relax_pad, 1, length + 1, axis_dim)
    )
    edges = (2.0 * relax_face * upwind + 0.5 * time_step * temp_face) / (
        2.0 * relax_face + 0.5 * time_step
    )
    return along_speed * (window(edges, 1, length, axis_dim) - window(edges, 0, length, axis_dim))


def spread(flux_x_pad, flux_y_pad, flux_z):
    flux_z_pad = jnp.pad(flux_z, ((0, 0), (0, 0), (1, 1)))
    result = 0.5 * (flux_x_pad[2:, 1:-1, 1:-1] - flux_x_pad[:-2, 1:-1, 1:-1])
    result = result + 0.5 * (flux_y_pad[1:-1, 2:, 1:-1] - flux_y_pad[1:-1, :-2, 1:-1])
    return result + 0.5 * (flux_z_pad[:, :, 2:] - flux_z_pad[:, :, :-2])


def relax_sweep(potential_pad, driver):
    conduct = 1.0 / (1.0 + potential_pad * potential_pad)
    centre = conduct[1:-1, 1:-1, 1:-1]
    weighted = diffusion_mass * driver
    weights = diffusion_mass + jnp.zeros_like(driver)
    for axis_dim in range(3):
        for anchor in (0, 2):
            picker = tuple(
                (
                    (
                        slice(anchor, anchor + potential_pad.shape[axis_dim] - 2)
                        if dimension == axis_dim
                        else slice(1, -1)
                    )
                    for dimension in range(3)
                )
            )
            couple = 0.5 * (centre + conduct[picker])
            weighted = weighted + couple * potential_pad[picker]
            weights = weights + couple
    return weighted / weights


def transport(current, local_temp, relax, speeds):
    source = source_of(current, local_temp, relax)
    ordinal_rows = source.shape[0]
    stacked = jnp.concatenate([source, local_temp[None], relax[None]], 0)
    widened = extended(stacked, (("gx", 1), ("gy", 2)), 2)
    along_x = widened[:, :, 2:-2, :]
    along_y = widened[:, 2:-2, :, :]
    fluxes = axis_flux(
        along_x[:ordinal_rows],
        along_x[ordinal_rows : ordinal_rows + 1, 1:-1],
        along_x[ordinal_rows + 1 :, 1:-1],
        speeds[0][:, None, None, None],
        1,
    )
    fluxes = fluxes + axis_flux(
        along_y[:ordinal_rows],
        along_y[ordinal_rows : ordinal_rows + 1, :, 1:-1],
        along_y[ordinal_rows + 1 :, :, 1:-1],
        speeds[1][:, None, None, None],
        2,
    )
    fluxes = fluxes + axis_flux(
        pad_along(source, 2, 3),
        pad_along(local_temp[None], 1, 3),
        pad_along(relax[None], 1, 3),
        speeds[2][:, None, None, None],
        3,
    )
    return source - time_step * fluxes


def block_extend(stacked):
    widened = extended(stacked, (("gx", 1), ("gy", 2)), 1)
    return jnp.pad(widened, ((0, 0), (0, 0), (0, 0), (1, 1)))


def diffuse(shares, extend):
    energy = shares[0]
    widened = extend(shares[:3])
    driver = energy - flux_weight * spread(widened[1], widened[2], shares[3])
    potential = relax_sweep(widened[0], driver)
    for rounds in range(1, SWEEPS):
        potential = relax_sweep(extend(potential[None])[0], driver)
    return potential


def local(distribution, relaxation):
    local_count = distribution.shape[0]
    speeds = directions(lax.axis_index("ord") * local_count, local_count)
    current = distribution
    for repeat in range(STEPS):
        local_temp = lax.psum(jnp.sum(current, 0) / NORD, "ord")
        current = transport(current, local_temp, relaxation, speeds)
    partial_value = (
        jnp.concatenate(
            [jnp.sum(current, 0)[None], jnp.sum(speeds[:, :, None, None, None] * current[None], 1)],
            0,
        )
        / NORD
    )
    shares = lax.psum(partial_value, "ord")
    potential = diffuse(shares, block_extend)
    updated = source_of(current, potential, relaxation)
    return (updated, potential)


def solution(mesh):
    placed = (P("ord", "gx", "gy", None), P("gx", "gy", None))
    return jax.shard_map(
        local,
        mesh=mesh,
        in_specs=placed,
        out_specs=(P("ord", "gx", "gy", None), P("gx", "gy", None)),
        check_vma=False,
    )
```

profile of v0, /device:TPU:0, one launch (start us, length us, event | category | flops | bytes accessed | tf_op | source)
XLA Modules:
  0.0 365.7 jit_solution(15019233585724942882)
XLA Ops:
  7.2 2.0 reduce_sum.36
  12.2 56.1 %all-reduce.13.cloned.1.call-done = f32[32,4,128]{2,1,0:T(4,128)} async-done(((f32[32,4,128]{2,1,0:T(4,128)}), f32[32,4,128]{2,1,0:T(4,128)}) %all-reduce.13.cloned.1.call-update) | async-done | bytes 65552 | tf_op jit(solution)/shard_map/psum | solution.py:167
  71.5 2.4 add_divide_fusion.1
  74.3 3.4 collective-permute-start
  79.0 2.6 fusion.4
  81.5 3.0 collective-permute-done.1
  85.2 3.5 collective-permute-start.2
  93.6 21.6 %collective-permute-done.2 = f32[34,36,2,128]{3,1,2,0:T(8,128)S(1)} collective-permute-done((f32[34,36,2,128]{3,1,2,0:T(8,128)S(1)}, f32[34,36,2,128]{3,1,2,0:T(8,128)S(1)}, u32[]{:S(2)}, u32[]{:S(2)}) %collective-permute-start.2) | collective-permute-done | bytes 1253408 | tf_op jit(solution)/shard_map/ppermute | solution.py:24
  115.3 4.2 %collective-permute-done.3 = f32[34,36,2,128]{3,1,2,0:T(8,128)S(1)} collective-permute-done((f32[34,36,2,128]{3,1,2,0:T(8,128)S(1)}, f32[34,36,2,128]{3,1,2,0:T(8,128)S(1)}, u32[]{:S(2)}, u32[]{:S(2)}) %collective-permute-start.3) | collective-permute-done | bytes 1253408 | tf_op jit(solution)/shard_map/ppermute | solution.py:26
  119.5 3.6 fusion.18
  123.1 3.5 add_divide_fusion.3
  131.0 53.0 %all-reduce.15.cloned.1.call-done = f32[32,4,128]{2,1,0:T(4,128)} async-done(((f32[32,4,128]{2,1,0:T(4,128)}), f32[32,4,128]{2,1,0:T(4,128)}) %all-reduce.15.cloned.1.call-update) | async-done | bytes 65552 | tf_op jit(solution)/shard_map/psum | solution.py:167
  187.1 2.4 add_divide_fusion
  189.8 3.4 collective-permute-start.4
  194.8 2.6 fusion.12
  197.4 2.8 collective-permute-done.5
  200.8 3.5 collective-permute-start.6
  209.1 21.8 %collective-permute-done.6 = f32[34,36,2,128]{3,1,2,0:T(8,128)S(1)} collective-permute-done((f32[34,36,2,128]{3,1,2,0:T(8,128)S(1)}, f32[34,36,2,128]{3,1,2,0:T(8,128)S(1)}, u32[]{:S(2)}, u32[]{:S(2)}) %collective-permute-start.6) | collective-permute-done | bytes 1253408 | tf_op jit(solution)/shard_map/ppermute | solution.py:24
  230.9 4.2 %collective-permute-done.7 = f32[34,36,2,128]{3,1,2,0:T(8,128)S(1)} collective-permute-done((f32[34,36,2,128]{3,1,2,0:T(8,128)S(1)}, f32[34,36,2,128]{3,1,2,0:T(8,128)S(1)}, u32[]{:S(2)}, u32[]{:S(2)}) %collective-permute-start.7) | collective-permute-done | bytes 1253408 | tf_op jit(solution)/shard_map/ppermute | solution.py:26
  235.1 3.6 fusion.21
  238.7 3.5 add_divide_fusion.2
  243.9 1.8 fusion.156
  248.7 53.9 %all-reduce.17.cloned.1.call-done = f32[4,32,4,128]{3,2,1,0:T(4,128)} async-done(((f32[4,32,4,128]{3,2,1,0:T(4,128)}), f32[4,32,4,128]{3,2,1,0:T(4,128)}) %all-reduce.17.cloned.1.call-update) | async-done | bytes 262160 | tf_op jit(solution)/shard_map/psum | solution.py:176
  303.2 3.4 collective-permute-start.8
  308.9 3.3 collective-permute-done.9
  312.2 3.4 collective-permute-start.10
  318.0 3.6 collective-permute-done.11
  327.1 4.2 %collective-permute-done.13 = f32[1,1,4,128]{3,2,1,0:T(4,128)S(1)} collective-permute-done((f32[1,1,4,128]{3,2,1,0:T(4,128)S(1)}, f32[1,1,4,128]{3,2,1,0:T(4,128)S(1)}, u32[]{:S(2)}, u32[]{:S(2)}) %collective-permute-start.13) | collective-permute-done | bytes 2080 | tf_op jit(solution)/shard_map/ppermute | solution.py:26
  334.3 4.2 %collective-permute-done.15 = f32[1,34,1,128]{3,2,1,0:T(1,128)S(1)} collective-permute-done((f32[1,34,1,128]{3,2,1,0:T(1,128)S(1)}, f32[1,34,1,128]{3,2,1,0:T(1,128)S(1)}, u32[]{:S(2)}, u32[]{:S(2)}) %collective-permute-start.15) | collective-permute-done | bytes 17440 | tf_op jit(solution)/shard_map/ppermute | solution.py:26
  342.6 4.2 %collective-permute-done.17 = f32[1,1,4,128]{3,2,1,0:T(4,128)S(1)} collective-permute-done((f32[1,1,4,128]{3,2,1,0:T(4,128)S(1)}, f32[1,1,4,128]{3,2,1,0:T(4,128)S(1)}, u32[]{:S(2)}, u32[]{:S(2)}) %collective-permute-start.17) | collective-permute-done | bytes 2080 | tf_op jit(solution)/shard_map/ppermute | solution.py:26
  349.8 4.2 %collective-permute-done.19 = f32[1,34,1,128]{3,2,1,0:T(1,128)S(1)} collective-permute-done((f32[1,34,1,128]{3,2,1,0:T(1,128)S(1)}, f32[1,34,1,128]{3,2,1,0:T(1,128)S(1)}, u32[]{:S(2)}, u32[]{:S(2)}) %collective-permute-start.19) | collective-permute-done | bytes 17440 | tf_op jit(solution)/shard_map/ppermute | solution.py:26
  356.1 3.1 copy.53
  (110 shorter events, 55.5 us)
Async XLA Ops:
  7.2 63.9 %copy-start = (f32[32,32,4,128]{3,2,1,0:T(4,128)S(1)}, f32[32,32,4,128]{3,2,1,0:T(4,128)}, u32[]{:S(2)}) copy-start(f32[32,32,4,128]{3,2,1,0:T(4,128)} %param.2) | copy-start | bytes 6291460
  7.2 61.1 %all-reduce.13.cloned.1.call-start = ((), (), s32[]{:S(2)}) async-start(), calls=%async_computation | async-start | bytes 131072 | tf_op jit(solution)/shard_map/psum | solution.py:167
  9.9 174.1 %all-reduce.15.cloned.1.call-start = ((), (), s32[]{:S(2)}) async-start(), calls=%async_computation.1 | async-start | bytes 131072 | tf_op jit(solution)/shard_map/psum | solution.py:167
  74.3 7.3 %collective-permute-start = (f32[34,2,4,128]{3,1,2,0:T(2,128)S(1)}, f32[34,2,4,128]{3,1,2,0:T(2,128)S(1)}, u32[]{:S(2)}, u32[]{:S(2)}) collective-permute-start(f32[34,2,4,128]{3,1,2,0:T(2,128)S(1)} %get-tuple-element.44), channel_id=1, source_target_pairs={{0,2},{1,3},{4,6},{5,7},{8,10},{9,11},{12,14},{13,15},{16,18},{17,... | collective-permute-start | bytes 417800 | tf_op jit(solution)/shard_map/ppermute | solution.py:24
  77.6 6.9 %collective-permute-start.1 = (f32[34,2,4,128]{3,1,2,0:T(2,128)S(1)}, f32[34,2,4,128]{3,1,2,0:T(2,128)S(1)}, u32[]{:S(2)}, u32[]{:S(2)}) collective-permute-start(f32[34,2,4,128]{3,1,2,0:T(2,128)S(1)} %get-tuple-element.45), channel_id=1, source_target_pairs={{2,0},{3,1},{6,4},{7,5},{10,8},{11,9},{14,12},{15,13},{18,16},{19,... | collective-permute-start | bytes 417800 | tf_op jit(solution)/shard_map/ppermute | solution.py:26
  85.2 30.0 %collective-permute-start.2 = (f32[34,36,2,128]{3,1,2,0:T(8,128)S(1)}, f32[34,36,2,128]{3,1,2,0:T(8,128)S(1)}, u32[]{:S(2)}, u32[]{:S(2)}) collective-permute-start(f32[34,36,2,128]{3,1,2,0:T(8,128)S(1)} %get-tuple-element.33), channel_id=1, source_target_pairs={{0,1},{2,3},{4,5},{6,7},{8,9},{10,11},{12,13},{14,15},{16,17},{18,... | collective-permute-start | bytes 3760136 | tf_op jit(solution)/shard_map/ppermute | solution.py:24
  88.7 30.7 %collective-permute-start.3 = (f32[34,36,2,128]{3,1,2,0:T(8,128)S(1)}, f32[34,36,2,128]{3,1,2,0:T(8,128)S(1)}, u32[]{:S(2)}, u32[]{:S(2)}) collective-permute-start(f32[34,36,2,128]{3,1,2,0:T(8,128)S(1)} %get-tuple-element.32), channel_id=1, source_target_pairs={{1,0},{3,2},{5,4},{7,6},{9,8},{11,10},{13,12},{15,14},{17,16},{19,... | collective-permute-start | bytes 3760136 | tf_op jit(solution)/shard_map/ppermute | solution.py:26
  126.6 1.8 copy-start.1
  130.9 171.6 %all-reduce.17.cloned.1.call-start = ((), (), s32[]{:S(2)}) async-start(), calls=%async_computation.2 | async-start | bytes 524288 | tf_op jit(solution)/shard_map/psum | solution.py:176
  189.8 7.5 %collective-permute-start.4 = (f32[34,2,4,128]{3,1,2,0:T(2,128)S(1)}, f32[34,2,4,128]{3,1,2,0:T(2,128)S(1)}, u32[]{:S(2)}, u32[]{:S(2)}) collective-permute-start(f32[34,2,4,128]{3,1,2,0:T(2,128)S(1)} %get-tuple-element.40), channel_id=1, source_target_pairs={{0,2},{1,3},{4,6},{5,7},{8,10},{9,11},{12,14},{13,15},{16,18},{17,... | collective-permute-start | bytes 417800 | tf_op jit(solution)/shard_map/ppermute | solution.py:24
  193.2 6.9 %collective-permute-start.5 = (f32[34,2,4,128]{3,1,2,0:T(2,128)S(1)}, f32[34,2,4,128]{3,1,2,0:T(2,128)S(1)}, u32[]{:S(2)}, u32[]{:S(2)}) collective-permute-start(f32[34,2,4,128]{3,1,2,0:T(2,128)S(1)} %get-tuple-element.41), channel_id=1, source_target_pairs={{2,0},{3,1},{6,4},{7,5},{10,8},{11,9},{14,12},{15,13},{18,16},{19,... | collective-permute-start | bytes 417800 | tf_op jit(solution)/shard_map/ppermute | solution.py:26
  200.8 30.0 %collective-permute-start.6 = (f32[34,36,2,128]{3,1,2,0:T(8,128)S(1)}, f32[34,36,2,128]{3,1,2,0:T(8,128)S(1)}, u32[]{:S(2)}, u32[]{:S(2)}) collective-permute-start(f32[34,36,2,128]{3,1,2,0:T(8,128)S(1)} %get-tuple-element.31), channel_id=1, source_target_pairs={{0,1},{2,3},{4,5},{6,7},{8,9},{10,11},{12,13},{14,15},{16,17},{18,... | collective-permute-start | bytes 3760136 | tf_op jit(solution)/shard_map/ppermute | solution.py:24
  204.3 30.7 %collective-permute-start.7 = (f32[34,36,2,128]{3,1,2,0:T(8,128)S(1)}, f32[34,36,2,128]{3,1,2,0:T(8,128)S(1)}, u32[]{:S(2)}, u32[]{:S(2)}) collective-permute-start(f32[34,36,2,128]{3,1,2,0:T(8,128)S(1)} %get-tuple-element.30), channel_id=1, source_target_pairs={{1,0},{3,2},{5,4},{7,6},{9,8},{11,10},{13,12},{15,14},{17,16},{19,... | collective-permute-start | bytes 3760136 | tf_op jit(solution)/shard_map/ppermute | solution.py:26
  245.8 1.3 copy-start.2
  303.2 5.6 %collective-permute-start.8 = (f32[3,1,4,128]{3,2,1,0:T(4,128)S(1)}, f32[3,1,4,128]{3,2,1,0:T(4,128)S(1)}, u32[]{:S(2)}, u32[]{:S(2)}) collective-permute-start(f32[3,1,4,128]{3,2,1,0:T(4,128)S(1)} %get-tuple-element.49), channel_id=1, source_target_pairs={{0,2},{1,3},{4,6},{5,7},{8,10},{9,11},{12,14},{13,15},{16,18},{17,... | collective-permute-start | bytes 18440 | tf_op jit(solution)/shard_map/ppermute | solution.py:24
  306.6 5.5 %collective-permute-start.9 = (f32[3,1,4,128]{3,2,1,0:T(4,128)S(1)}, f32[3,1,4,128]{3,2,1,0:T(4,128)S(1)}, u32[]{:S(2)}, u32[]{:S(2)}) collective-permute-start(f32[3,1,4,128]{3,2,1,0:T(4,128)S(1)} %get-tuple-element.50), channel_id=1, source_target_pairs={{2,0},{3,1},{6,4},{7,5},{10,8},{11,9},{14,12},{15,13},{18,16},{19,... | collective-permute-start | bytes 18440 | tf_op jit(solution)/shard_map/ppermute | solution.py:26
  312.2 5.8 %collective-permute-start.10 = (f32[3,34,1,128]{3,2,1,0:T(1,128)S(1)}, f32[3,34,1,128]{3,2,1,0:T(1,128)S(1)}, u32[]{:S(2)}, u32[]{:S(2)}) collective-permute-start(f32[3,34,1,128]{3,2,1,0:T(1,128)S(1)} %get-tuple-element.51), channel_id=1, source_target_pairs={{0,1},{2,3},{4,5},{6,7},{8,9},{10,11},{12,13},{14,15},{16,17},{18,... | collective-permute-start | bytes 156680 | tf_op jit(solution)/shard_map/ppermute | solution.py:24
  315.6 6.0 %collective-permute-start.11 = (f32[3,34,1,128]{3,2,1,0:T(1,128)S(1)}, f32[3,34,1,128]{3,2,1,0:T(1,128)S(1)}, u32[]{:S(2)}, u32[]{:S(2)}) collective-permute-start(f32[3,34,1,128]{3,2,1,0:T(1,128)S(1)} %get-tuple-element.52), channel_id=1, source_target_pairs={{1,0},{3,2},{5,4},{7,6},{9,8},{11,10},{13,12},{15,14},{17,16},{19,... | collective-permute-start | bytes 156680 | tf_op jit(solution)/shard_map/ppermute | solution.py:26
  322.5 33.3 %copy-start.3 = (f32[32,32,4,128]{3,1,2,0:T(8,128)S(1)}, f32[32,32,4,128]{3,1,2,0:T(8,128)}, u32[]{:S(2)}) copy-start(f32[32,32,4,128]{3,1,2,0:T(8,128)} %copy-done.2) | copy-start | bytes 6291460
  324.1 3.0 collective-permute-start.12
  325.8 5.5 %collective-permute-start.13 = (f32[1,1,4,128]{3,2,1,0:T(4,128)S(1)}, f32[1,1,4,128]{3,2,1,0:T(4,128)S(1)}, u32[]{:S(2)}, u32[]{:S(2)}) collective-permute-start(f32[1,1,4,128]{3,2,1,0:T(4,128)S(1)} %get-tuple-element.60), channel_id=1, source_target_pairs={{2,0},{3,1},{6,4},{7,5},{10,8},{11,9},{14,12},{15,13},{18,16},{19,... | collective-permute-start | bytes 6152 | tf_op jit(solution)/shard_map/ppermute | solution.py:26
  331.3 3.0 collective-permute-start.14
  332.9 5.6 %collective-permute-start.15 = (f32[1,34,1,128]{3,2,1,0:T(1,128)S(1)}, f32[1,34,1,128]{3,2,1,0:T(1,128)S(1)}, u32[]{:S(2)}, u32[]{:S(2)}) collective-permute-start(f32[1,34,1,128]{3,2,1,0:T(1,128)S(1)} %get-tuple-element.56), channel_id=1, source_target_pairs={{1,0},{3,2},{5,4},{7,6},{9,8},{11,10},{13,12},{15,14},{17,16},{19,... | collective-permute-start | bytes 52232 | tf_op jit(solution)/shard_map/ppermute | solution.py:26
  339.6 3.0 collective-permute-start.16
  341.2 5.5 %collective-permute-start.17 = (f32[1,1,4,128]{3,2,1,0:T(4,128)S(1)}, f32[1,1,4,128]{3,2,1,0:T(4,128)S(1)}, u32[]{:S(2)}, u32[]{:S(2)}) collective-permute-start(f32[1,1,4,128]{3,2,1,0:T(4,128)S(1)} %get-tuple-element.58), channel_id=1, source_target_pairs={{2,0},{3,1},{6,4},{7,5},{10,8},{11,9},{14,12},{15,13},{18,16},{19,... | collective-permute-start | bytes 6152 | tf_op jit(solution)/shard_map/ppermute | solution.py:26
  346.8 3.1 collective-permute-start.18
  348.4 5.6 %collective-permute-start.19 = (f32[1,34,1,128]{3,2,1,0:T(1,128)S(1)}, f32[1,34,1,128]{3,2,1,0:T(1,128)S(1)}, u32[]{:S(2)}, u32[]{:S(2)}) collective-permute-start(f32[1,34,1,128]{3,2,1,0:T(1,128)S(1)} %get-tuple-element.54), channel_id=1, source_target_pairs={{1,0},{3,2},{5,4},{7,6},{9,8},{11,10},{13,12},{15,14},{17,16},{19,... | collective-permute-start | bytes 52232 | tf_op jit(solution)/shard_map/ppermute | solution.py:26
Sparse Core Ops, SparseCore 0:
  10.9 57.4 all-reduce.12
  131.0 52.9 all-reduce.14
  248.8 53.7 all-reduce.16
where the time goes:
time: 367 us; the launch traced here: 366 us
  waiting for transfers between devices  245 us (67%)
  other arithmetic  55.6 us (15%)
  starting transfers between devices  40.7 us (11%)
  between operations  14.5 us (4%)
  local copies, waits for them, and re-layouts  10.4 us (3%)
    psum x2, waiting for transfers between devices, local(): local_temp = lax.psum(jnp.sum(current, 0) / NORD, 'ord')  109 us
    psum x1, waiting for transfers between devices, local(): shares = lax.psum(partial_value, 'ord')  53.9 us
    ppermute x10, waiting for transfers between devices, extended(): lax.ppermute(tail, axis, [(i, (i + 1) % count) for i in range(ends)])  43.7 us
    ppermute x10, waiting for transfers between devices, extended(): lax.ppermute(head, axis, [((i + 1) % count, i) for i in range(ends)])  37.9 us
    ppermute x10, starting transfers between devices, extended(): lax.ppermute(tail, axis, [(i, (i + 1) % count) for i in range(ends)])  27 us
    div x6, other arithmetic, axis_flux(): (lower_diff * (upper_diff * upper_diff + limiter_eps) + upper_diff * (low...  14.3 us
    ppermute x10, starting transfers between devices, extended(): lax.ppermute(head, axis, [((i + 1) % count, i) for i in range(ends)])  13.6 us
    div x6, other arithmetic, axis_flux(): (2.0 * relax_face * upwind + 0.5 * time_step * temp_face) / (2.0 * relax_...  11.4 us
  transfers between devices with their start and end apart: 23, of which 17 were waited for; matrix products, arithmetic and copies ran while one was open for 4% of the time, Pallas kernels for 0%

commit v1 on v0

--- a/solution.py
+++ b/solution.py
@@ -173,7 +173,9 @@
         )
         / NORD
     )
-    shares = lax.psum(partial_value, "ord")
+    shares = partial_value
+    for hop in (1, 2, 4):
+        shares = shares + lax.ppermute(shares, "ord", [(dev, dev ^ hop) for dev in range(8)])
     potential = diffuse(shares, block_extend)
     updated = source_of(current, potential, relaxation)
     return (updated, potential)

time: 367 us -> 331 us (0.902)
  waiting for transfers between devices: 245 us -> 215 us
  local copies, waits for them, and re-layouts: 10.4 us -> 6.56 us
    psum x1 -> x0, waiting for transfers between devices: 53.9 us -> none  [local(): shares = lax.psum(partial_value, 'ord')]
    ppermute x0 -> x3, waiting for transfers between devices: none -> 21.8 us  [local(): lax.ppermute(shares, 'ord', [(dev, dev ^ hop) for dev in range(8)])]
  transfers between devices with their start and end apart: 23 -> 25, of which waited for: 17 -> 19; matrix products, arithmetic and copies ran while one was open for 4% -> 4% of each run, Pallas kernels for 0% -> 0%
where the time goes in v1:
time: 331 us; the launch traced here: 330 us
  waiting for transfers between devices  215 us (65%)
  other arithmetic  54.1 us (16%)
  starting transfers between devices  40 us (12%)
  between operations  14.8 us (4%)
  local copies, waits for them, and re-layouts  6.56 us (2%)
    psum x2, waiting for transfers between devices, local(): local_temp = lax.psum(jnp.sum(current, 0) / NORD, 'ord')  109 us
    ppermute x10, waiting for transfers between devices, extended(): lax.ppermute(tail, axis, [(i, (i + 1) % count) for i in range(ends)])  44 us
    ppermute x10, waiting for transfers between devices, extended(): lax.ppermute(head, axis, [((i + 1) % count, i) for i in range(ends)])  39.6 us
    ppermute x10, starting transfers between devices, extended(): lax.ppermute(tail, axis, [(i, (i + 1) % count) for i in range(ends)])  24.3 us
    ppermute x3, waiting for transfers between devices, local(): lax.ppermute(shares, 'ord', [(dev, dev ^ hop) for dev in range(8)])  21.8 us
    div x6, other arithmetic, axis_flux(): (lower_diff * (upper_diff * upper_diff + limiter_eps) + upper_diff * (low...  14.3 us
    ppermute x10, starting transfers between devices, extended(): lax.ppermute(head, axis, [((i + 1) % count, i) for i in range(ends)])  13.4 us
    div x6, other arithmetic, axis_flux(): (2.0 * relax_face * upwind + 0.5 * time_step * temp_face) / (2.0 * relax_...  11.4 us
  transfers between devices with their start and end apart: 25, of which 19 were waited for; matrix products, arithmetic and copies ran while one was open for 4% of the time, Pallas kernels for 0%

profile of v1, /device:TPU:0, one launch (start us, length us, event | category | flops | bytes accessed | tf_op | source)
XLA Modules:
  0.0 330.0 jit_solution(4430188509595245523)
XLA Ops:
  7.2 2.0 reduce_sum.36
  12.2 56.1 %all-reduce.12.cloned.1.call-done = f32[32,4,128]{2,1,0:T(4,128)} async-done(((f32[32,4,128]{2,1,0:T(4,128)}), f32[32,4,128]{2,1,0:T(4,128)}) %all-reduce.12.cloned.1.call-update) | async-done | bytes 65552 | tf_op jit(solution)/shard_map/psum | solution.py:167
  71.5 2.4 add_divide_fusion.1
  74.3 3.4 %collective-permute-start = (f32[34,2,4,128]{3,1,2,0:T(2,128)S(1)}, f32[34,2,4,128]{3,1,2,0:T(2,128)S(1)}, u32[]{:S(2)}, u32[]{:S(2)}) collective-permute-start(f32[34,2,4,128]{3,1,2,0:T(2,128)S(1)} %get-tuple-element.44), channel_id=1, source_target_pairs={{0,2},{1,3},{4,6},{5,7},{8,10},{9,11},{12,14},{13,15},{16,18},{17,... | collective-permute-start | bytes 417800 | tf_op jit(solution)/shard_map/ppermute | solution.py:24
  79.0 2.6 fusion.4
  81.5 3.0 collective-permute-done.1
  85.2 3.5 %collective-permute-start.2 = (f32[34,36,2,128]{3,1,2,0:T(8,128)S(1)}, f32[34,36,2,128]{3,1,2,0:T(8,128)S(1)}, u32[]{:S(2)}, u32[]{:S(2)}) collective-permute-start(f32[34,36,2,128]{3,1,2,0:T(8,128)S(1)} %get-tuple-element.33), channel_id=1, source_target_pairs={{0,1},{2,3},{4,5},{6,7},{8,9},{10,11},{12,13},{14,15},{16,17},{18,... | collective-permute-start | bytes 3760136 | tf_op jit(solution)/shard_map/ppermute | solution.py:24
  93.6 21.6 %collective-permute-done.2 = f32[34,36,2,128]{3,1,2,0:T(8,128)S(1)} collective-permute-done((f32[34,36,2,128]{3,1,2,0:T(8,128)S(1)}, f32[34,36,2,128]{3,1,2,0:T(8,128)S(1)}, u32[]{:S(2)}, u32[]{:S(2)}) %collective-permute-start.2) | collective-permute-done | bytes 1253408 | tf_op jit(solution)/shard_map/ppermute | solution.py:24
  115.3 4.2 %collective-permute-done.3 = f32[34,36,2,128]{3,1,2,0:T(8,128)S(1)} collective-permute-done((f32[34,36,2,128]{3,1,2,0:T(8,128)S(1)}, f32[34,36,2,128]{3,1,2,0:T(8,128)S(1)}, u32[]{:S(2)}, u32[]{:S(2)}) %collective-permute-start.3) | collective-permute-done | bytes 1253408 | tf_op jit(solution)/shard_map/ppermute | solution.py:26
  119.5 3.6 %fusion.18 = (f32[34,36,6,128]{3,1,2,0:T(8,128)S(1)}, f32[34,36,6,128]{3,1,2,0:T(8,128)S(1)}) fusion(f32[1,32,4,128]{3,1,2,0:T(8,128)S(1)} %bitcast.71, f32[34,36,2,128]{3,1,2,0:T(8,128)S(1)} %collective-permute-done.3, f32[34,2,4,128]{3,1,2,0:T(2,128)S(1)} %collective-permute-done.1, f32[1,32,4,128]{3,1,2,0:T(8,128)S(1)} %copy.44, ...), kind=kLoop, calls=%fused_computation.41 | loop fusion | flops 9400320 | bytes 12533760 | tf_op jit(solution)/shard_map/concatenate | solution.py:22
  123.1 3.5 %add_divide_fusion.3 = f32[32,32,6,128]{3,1,2,0:T(8,128)S(1)} fusion(f32[34,36,6,128]{3,1,2,0:T(8,128)S(1)} %get-tuple-element.37, f32[34,36,6,128]{3,1,2,0:T(8,128)S(1)} %get-tuple-element.36, f32[34,36,2,128]{3,1,2,0:T(8,128)S(1)} %collective-permute-done.3, f32[34,2,4,128]{3,1,2,0:T(2,128)S(1)} %collective-permute-done.1, ...), kind=kLoop, calls=%fused_computation.74 | loop fusion | flops 14155776 | bytes 14450688 | tf_op jit(solution)/shard_map/div | solution.py:63
  130.9 53.1 %all-reduce.14.cloned.1.call-done = f32[32,4,128]{2,1,0:T(4,128)} async-done(((f32[32,4,128]{2,1,0:T(4,128)}), f32[32,4,128]{2,1,0:T(4,128)}) %all-reduce.14.cloned.1.call-update) | async-done | bytes 65552 | tf_op jit(solution)/shard_map/psum | solution.py:167
  187.1 2.4 add_divide_fusion
  189.8 3.4 %collective-permute-start.4 = (f32[34,2,4,128]{3,1,2,0:T(2,128)S(1)}, f32[34,2,4,128]{3,1,2,0:T(2,128)S(1)}, u32[]{:S(2)}, u32[]{:S(2)}) collective-permute-start(f32[34,2,4,128]{3,1,2,0:T(2,128)S(1)} %get-tuple-element.40), channel_id=1, source_target_pairs={{0,2},{1,3},{4,6},{5,7},{8,10},{9,11},{12,14},{13,15},{16,18},{17,... | collective-permute-start | bytes 417800 | tf_op jit(solution)/shard_map/ppermute | solution.py:24
  194.6 2.6 fusion.12
  197.1 3.0 collective-permute-done.5
  200.8 3.7 %collective-permute-start.6 = (f32[34,36,2,128]{3,1,2,0:T(8,128)S(1)}, f32[34,36,2,128]{3,1,2,0:T(8,128)S(1)}, u32[]{:S(2)}, u32[]{:S(2)}) collective-permute-start(f32[34,36,2,128]{3,1,2,0:T(8,128)S(1)} %get-tuple-element.31), channel_id=1, source_target_pairs={{0,1},{2,3},{4,5},{6,7},{8,9},{10,11},{12,13},{14,15},{16,17},{18,... | collective-permute-start | bytes 3760136 | tf_op jit(solution)/shard_map/ppermute | solution.py:24
  209.3 21.8 %collective-permute-done.6 = f32[34,36,2,128]{3,1,2,0:T(8,128)S(1)} collective-permute-done((f32[34,36,2,128]{3,1,2,0:T(8,128)S(1)}, f32[34,36,2,128]{3,1,2,0:T(8,128)S(1)}, u32[]{:S(2)}, u32[]{:S(2)}) %collective-permute-start.6) | collective-permute-done | bytes 1253408 | tf_op jit(solution)/shard_map/ppermute | solution.py:24
  231.1 4.2 %collective-permute-done.7 = f32[34,36,2,128]{3,1,2,0:T(8,128)S(1)} collective-permute-done((f32[34,36,2,128]{3,1,2,0:T(8,128)S(1)}, f32[34,36,2,128]{3,1,2,0:T(8,128)S(1)}, u32[]{:S(2)}, u32[]{:S(2)}) %collective-permute-start.7) | collective-permute-done | bytes 1253408 | tf_op jit(solution)/shard_map/ppermute | solution.py:26
  235.3 3.6 %fusion.21 = (f32[34,36,6,128]{3,1,2,0:T(8,128)S(1)}, f32[34,36,6,128]{3,1,2,0:T(8,128)S(1)}) fusion(f32[1,32,4,128]{3,1,2,0:T(8,128)S(1)} %bitcast.76, f32[34,36,2,128]{3,1,2,0:T(8,128)S(1)} %collective-permute-done.7, f32[34,2,4,128]{3,1,2,0:T(2,128)S(1)} %collective-permute-done.5, f32[1,32,4,128]{3,1,2,0:T(8,128)S(1)} %copy.48, ...), kind=kLoop, calls=%fused_computation.44 | loop fusion | flops 9400320 | bytes 12533760 | tf_op jit(solution)/shard_map/concatenate | solution.py:22
  238.9 3.5 %add_divide_fusion.2 = f32[32,32,6,128]{3,1,2,0:T(8,128)S(1)} fusion(f32[34,36,6,128]{3,1,2,0:T(8,128)S(1)} %get-tuple-element.35, f32[34,36,6,128]{3,1,2,0:T(8,128)S(1)} %get-tuple-element.34, f32[34,36,2,128]{3,1,2,0:T(8,128)S(1)} %collective-permute-done.7, f32[34,2,4,128]{3,1,2,0:T(2,128)S(1)} %collective-permute-done.5, ...), kind=kLoop, calls=%fused_computation.73 | loop fusion | flops 14155776 | bytes 14450688 | tf_op jit(solution)/shard_map/div | solution.py:63
  244.2 1.8 fusion.157
  249.5 7.5 %collective-permute-done.9 = f32[4,32,4,128]{3,2,1,0:T(4,128)S(1)} collective-permute-done((f32[4,32,4,128]{3,2,1,0:T(4,128)S(1)}, f32[4,32,4,128]{3,2,1,0:T(4,128)S(1)}, u32[]{:S(2)}, u32[]{:S(2)}) %collective-permute-start.9) | collective-permute-done | bytes 262176 | tf_op jit(solution)/shard_map/ppermute | solution.py:178
  258.3 12.8 %collective-permute-done.10 = f32[4,32,4,128]{3,2,1,0:T(4,128)S(1)} collective-permute-done((f32[4,32,4,128]{3,2,1,0:T(4,128)S(1)}, f32[4,32,4,128]{3,2,1,0:T(4,128)S(1)}, u32[]{:S(2)}, u32[]{:S(2)}) %collective-permute-start.10) | collective-permute-done | bytes 262176 | tf_op jit(solution)/shard_map/ppermute | solution.py:178
  271.2 2.4 collective-permute-start.11
  274.9 4.2 %collective-permute-done.12 = f32[3,1,4,128]{3,2,1,0:T(4,128)S(1)} collective-permute-done((f32[3,1,4,128]{3,2,1,0:T(4,128)S(1)}, f32[3,1,4,128]{3,2,1,0:T(4,128)S(1)}, u32[]{:S(2)}, u32[]{:S(2)}) %collective-permute-start.12) | collective-permute-done | bytes 6176 | tf_op jit(solution)/shard_map/ppermute | solution.py:26
  282.4 4.3 %collective-permute-done.14 = f32[3,34,1,128]{3,2,1,0:T(1,128)S(1)} collective-permute-done((f32[3,34,1,128]{3,2,1,0:T(1,128)S(1)}, f32[3,34,1,128]{3,2,1,0:T(1,128)S(1)}, u32[]{:S(2)}, u32[]{:S(2)}) %collective-permute-start.14) | collective-permute-done | bytes 52256 | tf_op jit(solution)/shard_map/ppermute | solution.py:26
  291.1 4.2 %collective-permute-done.16 = f32[1,1,4,128]{3,2,1,0:T(4,128)S(1)} collective-permute-done((f32[1,1,4,128]{3,2,1,0:T(4,128)S(1)}, f32[1,1,4,128]{3,2,1,0:T(4,128)S(1)}, u32[]{:S(2)}, u32[]{:S(2)}) %collective-permute-start.16) | collective-permute-done | bytes 2080 | tf_op jit(solution)/shard_map/ppermute | solution.py:26
  298.5 4.1 %collective-permute-done.18 = f32[1,34,1,128]{3,2,1,0:T(1,128)S(1)} collective-permute-done((f32[1,34,1,128]{3,2,1,0:T(1,128)S(1)}, f32[1,34,1,128]{3,2,1,0:T(1,128)S(1)}, u32[]{:S(2)}, u32[]{:S(2)}) %collective-permute-start.18) | collective-permute-done | bytes 17440 | tf_op jit(solution)/shard_map/ppermute | solution.py:26
  306.6 4.2 %collective-permute-done.20 = f32[1,1,4,128]{3,2,1,0:T(4,128)S(1)} collective-permute-done((f32[1,1,4,128]{3,2,1,0:T(4,128)S(1)}, f32[1,1,4,128]{3,2,1,0:T(4,128)S(1)}, u32[]{:S(2)}, u32[]{:S(2)}) %collective-permute-start.20) | collective-permute-done | bytes 2080 | tf_op jit(solution)/shard_map/ppermute | solution.py:26
  313.9 4.2 %collective-permute-done.22 = f32[1,34,1,128]{3,2,1,0:T(1,128)S(1)} collective-permute-done((f32[1,34,1,128]{3,2,1,0:T(1,128)S(1)}, f32[1,34,1,128]{3,2,1,0:T(1,128)S(1)}, u32[]{:S(2)}, u32[]{:S(2)}) %collective-permute-start.22) | collective-permute-done | bytes 17440 | tf_op jit(solution)/shard_map/ppermute | solution.py:26
  320.1 3.1 copy.53
  (112 shorter events, 55.6 us)
Async XLA Ops:
  7.2 63.9 %copy-start = (f32[32,32,4,128]{3,2,1,0:T(4,128)S(1)}, f32[32,32,4,128]{3,2,1,0:T(4,128)}, u32[]{:S(2)}) copy-start(f32[32,32,4,128]{3,2,1,0:T(4,128)} %param.2) | copy-start | bytes 6291460
  7.2 61.1 %all-reduce.12.cloned.1.call-start = ((), (), s32[]{:S(2)}) async-start(), calls=%async_computation | async-start | bytes 131072 | tf_op jit(solution)/shard_map/psum | solution.py:167
  9.9 174.0 %all-reduce.14.cloned.1.call-start = ((), (), s32[]{:S(2)}) async-start(), calls=%async_computation.1 | async-start | bytes 131072 | tf_op jit(solution)/shard_map/psum | solution.py:167
  74.3 7.3 %collective-permute-start = (f32[34,2,4,128]{3,1,2,0:T(2,128)S(1)}, f32[34,2,4,128]{3,1,2,0:T(2,128)S(1)}, u32[]{:S(2)}, u32[]{:S(2)}) collective-permute-start(f32[34,2,4,128]{3,1,2,0:T(2,128)S(1)} %get-tuple-element.44), channel_id=1, source_target_pairs={{0,2},{1,3},{4,6},{5,7},{8,10},{9,11},{12,14},{13,15},{16,18},{17,... | collective-permute-start | bytes 417800 | tf_op jit(solution)/shard_map/ppermute | solution.py:24
  77.6 6.9 %collective-permute-start.1 = (f32[34,2,4,128]{3,1,2,0:T(2,128)S(1)}, f32[34,2,4,128]{3,1,2,0:T(2,128)S(1)}, u32[]{:S(2)}, u32[]{:S(2)}) collective-permute-start(f32[34,2,4,128]{3,1,2,0:T(2,128)S(1)} %get-tuple-element.45), channel_id=1, source_target_pairs={{2,0},{3,1},{6,4},{7,5},{10,8},{11,9},{14,12},{15,13},{18,16},{19,... | collective-permute-start | bytes 417800 | tf_op jit(solution)/shard_map/ppermute | solution.py:26
  85.2 30.0 %collective-permute-start.2 = (f32[34,36,2,128]{3,1,2,0:T(8,128)S(1)}, f32[34,36,2,128]{3,1,2,0:T(8,128)S(1)}, u32[]{:S(2)}, u32[]{:S(2)}) collective-permute-start(f32[34,36,2,128]{3,1,2,0:T(8,128)S(1)} %get-tuple-element.33), channel_id=1, source_target_pairs={{0,1},{2,3},{4,5},{6,7},{8,9},{10,11},{12,13},{14,15},{16,17},{18,... | collective-permute-start | bytes 3760136 | tf_op jit(solution)/shard_map/ppermute | solution.py:24
  88.7 30.7 %collective-permute-start.3 = (f32[34,36,2,128]{3,1,2,0:T(8,128)S(1)}, f32[34,36,2,128]{3,1,2,0:T(8,128)S(1)}, u32[]{:S(2)}, u32[]{:S(2)}) collective-permute-start(f32[34,36,2,128]{3,1,2,0:T(8,128)S(1)} %get-tuple-element.32), channel_id=1, source_target_pairs={{1,0},{3,2},{5,4},{7,6},{9,8},{11,10},{13,12},{15,14},{17,16},{19,... | collective-permute-start | bytes 3760136 | tf_op jit(solution)/shard_map/ppermute | solution.py:26
  126.6 1.8 copy-start.1
  189.8 7.3 %collective-permute-start.4 = (f32[34,2,4,128]{3,1,2,0:T(2,128)S(1)}, f32[34,2,4,128]{3,1,2,0:T(2,128)S(1)}, u32[]{:S(2)}, u32[]{:S(2)}) collective-permute-start(f32[34,2,4,128]{3,1,2,0:T(2,128)S(1)} %get-tuple-element.40), channel_id=1, source_target_pairs={{0,2},{1,3},{4,6},{5,7},{8,10},{9,11},{12,14},{13,15},{16,18},{17,... | collective-permute-start | bytes 417800 | tf_op jit(solution)/shard_map/ppermute | solution.py:24
  193.2 6.9 %collective-permute-start.5 = (f32[34,2,4,128]{3,1,2,0:T(2,128)S(1)}, f32[34,2,4,128]{3,1,2,0:T(2,128)S(1)}, u32[]{:S(2)}, u32[]{:S(2)}) collective-permute-start(f32[34,2,4,128]{3,1,2,0:T(2,128)S(1)} %get-tuple-element.41), channel_id=1, source_target_pairs={{2,0},{3,1},{6,4},{7,5},{10,8},{11,9},{14,12},{15,13},{18,16},{19,... | collective-permute-start | bytes 417800 | tf_op jit(solution)/shard_map/ppermute | solution.py:26
  200.8 30.2 %collective-permute-start.6 = (f32[34,36,2,128]{3,1,2,0:T(8,128)S(1)}, f32[34,36,2,128]{3,1,2,0:T(8,128)S(1)}, u32[]{:S(2)}, u32[]{:S(2)}) collective-permute-start(f32[34,36,2,128]{3,1,2,0:T(8,128)S(1)} %get-tuple-element.31), channel_id=1, source_target_pairs={{0,1},{2,3},{4,5},{6,7},{8,9},{10,11},{12,13},{14,15},{16,17},{18,... | collective-permute-start | bytes 3760136 | tf_op jit(solution)/shard_map/ppermute | solution.py:24
  204.5 30.7 %collective-permute-start.7 = (f32[34,36,2,128]{3,1,2,0:T(8,128)S(1)}, f32[34,36,2,128]{3,1,2,0:T(8,128)S(1)}, u32[]{:S(2)}, u32[]{:S(2)}) collective-permute-start(f32[34,36,2,128]{3,1,2,0:T(8,128)S(1)} %get-tuple-element.30), channel_id=1, source_target_pairs={{1,0},{3,2},{5,4},{7,6},{9,8},{11,10},{13,12},{15,14},{17,16},{19,... | collective-permute-start | bytes 3760136 | tf_op jit(solution)/shard_map/ppermute | solution.py:26
  246.8 1.6 collective-permute-start.8
  248.5 8.4 %collective-permute-start.9 = (f32[4,32,4,128]{3,2,1,0:T(4,128)S(1)}, f32[4,32,4,128]{3,2,1,0:T(4,128)S(1)}, u32[]{:S(2)}, u32[]{:S(2)}) collective-permute-start(f32[4,32,4,128]{3,2,1,0:T(4,128)S(1)} %fusion.154), channel_id=1, source_target_pairs={{0,8},{4,12},{8,0},{12,4},{16,24},{20,28},{24,16},{28,20},{1,9},{5... | collective-permute-start | bytes 786440 | tf_op jit(solution)/shard_map/ppermute | solution.py:178
  257.0 14.1 %collective-permute-start.10 = (f32[4,32,4,128]{3,2,1,0:T(4,128)S(1)}, f32[4,32,4,128]{3,2,1,0:T(4,128)S(1)}, u32[]{:S(2)}, u32[]{:S(2)}) collective-permute-start(f32[4,32,4,128]{3,2,1,0:T(4,128)S(1)} %add.694), channel_id=1, source_target_pairs={{0,16},{4,20},{8,24},{12,28},{16,0},{20,4},{24,8},{28,12},{1,17},{... | collective-permute-start | bytes 786440 | tf_op jit(solution)/shard_map/ppermute | solution.py:178
  271.2 3.7 %collective-permute-start.11 = (f32[3,1,4,128]{3,2,1,0:T(4,128)S(1)}, f32[3,1,4,128]{3,2,1,0:T(4,128)S(1)}, u32[]{:S(2)}, u32[]{:S(2)}) collective-permute-start(f32[3,1,4,128]{3,2,1,0:T(4,128)S(1)} %get-tuple-element.49), channel_id=1, source_target_pairs={{0,2},{1,3},{4,6},{5,7},{8,10},{9,11},{12,14},{13,15},{16,18},{17,... | collective-permute-start | bytes 18440 | tf_op jit(solution)/shard_map/ppermute | solution.py:24
  273.6 5.5 %collective-permute-start.12 = (f32[3,1,4,128]{3,2,1,0:T(4,128)S(1)}, f32[3,1,4,128]{3,2,1,0:T(4,128)S(1)}, u32[]{:S(2)}, u32[]{:S(2)}) collective-permute-start(f32[3,1,4,128]{3,2,1,0:T(4,128)S(1)} %get-tuple-element.50), channel_id=1, source_target_pairs={{2,0},{3,1},{6,4},{7,5},{10,8},{11,9},{14,12},{15,13},{18,16},{19,... | collective-permute-start | bytes 18440 | tf_op jit(solution)/shard_map/ppermute | solution.py:26
  279.2 3.2 collective-permute-start.13
  280.7 6.0 %collective-permute-start.14 = (f32[3,34,1,128]{3,2,1,0:T(1,128)S(1)}, f32[3,34,1,128]{3,2,1,0:T(1,128)S(1)}, u32[]{:S(2)}, u32[]{:S(2)}) collective-permute-start(f32[3,34,1,128]{3,2,1,0:T(1,128)S(1)} %get-tuple-element.52), channel_id=1, source_target_pairs={{1,0},{3,2},{5,4},{7,6},{9,8},{11,10},{13,12},{15,14},{17,16},{19,... | collective-permute-start | bytes 156680 | tf_op jit(solution)/shard_map/ppermute | solution.py:26
  288.2 3.0 collective-permute-start.15
  289.8 5.5 %collective-permute-start.16 = (f32[1,1,4,128]{3,2,1,0:T(4,128)S(1)}, f32[1,1,4,128]{3,2,1,0:T(4,128)S(1)}, u32[]{:S(2)}, u32[]{:S(2)}) collective-permute-start(f32[1,1,4,128]{3,2,1,0:T(4,128)S(1)} %get-tuple-element.60), channel_id=1, source_target_pairs={{2,0},{3,1},{6,4},{7,5},{10,8},{11,9},{14,12},{15,13},{18,16},{19,... | collective-permute-start | bytes 6152 | tf_op jit(solution)/shard_map/ppermute | solution.py:26
  295.3 3.2 collective-permute-start.17
  296.9 5.6 %collective-permute-start.18 = (f32[1,34,1,128]{3,2,1,0:T(1,128)S(1)}, f32[1,34,1,128]{3,2,1,0:T(1,128)S(1)}, u32[]{:S(2)}, u32[]{:S(2)}) collective-permute-start(f32[1,34,1,128]{3,2,1,0:T(1,128)S(1)} %get-tuple-element.56), channel_id=1, source_target_pairs={{1,0},{3,2},{5,4},{7,6},{9,8},{11,10},{13,12},{15,14},{17,16},{19,... | collective-permute-start | bytes 52232 | tf_op jit(solution)/shard_map/ppermute | solution.py:26
  303.6 3.0 collective-permute-start.19
  305.3 5.5 %collective-permute-start.20 = (f32[1,1,4,128]{3,2,1,0:T(4,128)S(1)}, f32[1,1,4,128]{3,2,1,0:T(4,128)S(1)}, u32[]{:S(2)}, u32[]{:S(2)}) collective-permute-start(f32[1,1,4,128]{3,2,1,0:T(4,128)S(1)} %get-tuple-element.58), channel_id=1, source_target_pairs={{2,0},{3,1},{6,4},{7,5},{10,8},{11,9},{14,12},{15,13},{18,16},{19,... | collective-permute-start | bytes 6152 | tf_op jit(solution)/shard_map/ppermute | solution.py:26
  310.8 3.1 collective-permute-start.21
  312.5 5.6 %collective-permute-start.22 = (f32[1,34,1,128]{3,2,1,0:T(1,128)S(1)}, f32[1,34,1,128]{3,2,1,0:T(1,128)S(1)}, u32[]{:S(2)}, u32[]{:S(2)}) collective-permute-start(f32[1,34,1,128]{3,2,1,0:T(1,128)S(1)} %get-tuple-element.54), channel_id=1, source_target_pairs={{1,0},{3,2},{5,4},{7,6},{9,8},{11,10},{13,12},{15,14},{17,16},{19,... | collective-permute-start | bytes 52232 | tf_op jit(solution)/shard_map/ppermute | solution.py:26
Sparse Core Ops, SparseCore 0:
  10.9 57.4 all-reduce.11
  131.0 52.9 all-reduce.13
